TPU v7x, 32 devices: a whole 2x2x4 slice. The times are simulated.
32 devices in a mesh: prow: 4 (over y, core), pcol: 8 (over z, x).
Axes of the slice: x: 2, y: 2, z: 4, core: 2. Of those that a mesh axis runs over, the one named last changes fastest.
Arguments:
- ainv: bfloat16 [8192, 8192], P('prow', 'pcol'), may hold values from -6 to 6
- panels: bfloat16 [3, 8192, 128], P(None, ('prow', 'pcol')), may hold values from -0.0625 to 0.0625
- structure: int32 [3, 64], replicated, may hold values from 0 to 1, as said below
- dinv: float32 [3, 128, 128], replicated, may hold values from -6 to 6
- couple: bfloat16 [2, 128, 128], replicated, may hold values from -0.5 to 0.5
Outputs:
- inv_panels: float32 [3, 8192, 128], P(None, ('prow', 'pcol'))
- inv_parent: float32 [2, 128, 128], replicated
- inv_diag: float32 [3, 128, 128], replicated
Inputs may be any that keep to these rules, and one draw needn't show every extreme that they name: Entries are 0 or 1; a block in the structure of step k+1 is also in that of step k.
All inputs are finite; a program needn't handle non-finite values.
Results may differ from a plain program's by a relative error of at most 0.0003.
Values may be sent and summed in bfloat16 or wider, within the bound.
No kernel may reach another device: no remote copies, remote signals or barrier semaphores. Data moves between devices by JAX's collectives and lax.ppermute only.
A program may use at most 64 MiB of HBM per device.

v0:
```python
import jax
import jax.numpy as jnp
from jax import lax
from jax.sharding import PartitionSpec as P


def broadcast(value, axis, source):
    kept = jnp.where(lax.axis_index(axis) == source, value, 0).astype(value.dtype)
    return lax.psum(kept, axis)


def shards(ainv, panels, structure, dinv, couple):
    high = lax.Precision.HIGHEST
    n_col = lax.axis_size("pcol")
    seg_rows = panels.shape[1]
    width_cols = panels.shape[2]
    sections = panels.shape[0]
    col_span = ainv.shape[1]
    height = ainv.shape[0]
    flat_index = lax.axis_index("prow") * n_col + lax.axis_index("pcol")
    row_ids = flat_index * seg_rows + jnp.arange(seg_rows, dtype=jnp.int32)
    block_ids = jnp.arange(structure.shape[1], dtype=jnp.int32)
    onehot = (row_ids[:, None] // width_cols == block_ids[None, :]).astype(jnp.float32)
    live_rows = jnp.einsum("rb,kb->kr", onehot, structure.astype(jnp.float32))
    factor = panels * live_rows[:, :, None].astype(jnp.bfloat16)
    column = lax.axis_index("pcol")
    offset = column * col_span % height
    owner = column * col_span // height
    products = []
    for section in range(sections):
        gathered = lax.all_gather(factor[section], "pcol", axis=0, tiled=True)
        wanted = lax.dynamic_slice_in_dim(gathered, offset, col_span, 0)
        received = broadcast(wanted, "prow", owner)

        def single_term(row_start, row_count, panel_cols=received):
            return jnp.dot(ainv, panel_cols, preferred_element_type=jnp.float32)

        products.append(
            lax.psum_scatter(
                single_term(jnp.int32(0), seg_rows * lax.axis_size("pcol")),
                "pcol",
                scatter_dimension=0,
                tiled=True,
            )
        )
    factor_wide = factor.astype(jnp.float32)
    couple_wide = couple.astype(jnp.float32)
    first_block = -products[0] * live_rows[0][:, None]
    first_local = jnp.dot(factor_wide[0].T, first_block, precision=high)
    diag_now = dinv[0] - lax.psum(first_local, ("prow", "pcol"))
    blocks_out = [first_block]
    diag_out = [diag_now]
    cross_out = []
    for section in range(1, sections):
        previous = blocks_out[-1]
        current = (
            -(products[section] + jnp.dot(previous, couple_wide[section - 1], precision=high))
            * live_rows[section][:, None]
        )
        own_term = jnp.dot(factor_wide[section].T, current, precision=high)
        cross_term = jnp.dot(previous.T, factor_wide[section], precision=high)
        own_sum, cross_sum = lax.psum((own_term, cross_term), ("prow", "pcol"))
        cross = -(cross_sum + jnp.dot(diag_now, couple_wide[section - 1], precision=high))
        diag_now = (
            dinv[section] - own_sum - jnp.dot(couple_wide[section - 1].T, cross, precision=high)
        )
        blocks_out.append(current)
        cross_out.append(cross)
        diag_out.append(diag_now)
    return (jnp.stack(blocks_out), jnp.stack(cross_out), jnp.stack(diag_out))


def solution(mesh):
    return jax.shard_map(
        shards,
        mesh=mesh,
        in_specs=(P("prow", "pcol"), P(None, ("prow", "pcol"), None), P(), P(), P()),
        out_specs=(P(None, ("prow", "pcol"), None), P(), P()),
        check_vma=False,
    )
```

profile of v0, /device:TPU:8, one launch (start us, length us, event | category | flops | bytes accessed | tf_op | source)
XLA Modules:
  0.0 495.4 jit_solution(17148334694424355662)
XLA Ops:
  7.2 0.0 all-reduce.7.cloned.1.call-start
  7.3 0.9 fusion.45
  8.2 1.1 broadcast_multiply_fusion
  9.3 28.8 %all-gather = bf16[1,2048,128]{2,1,0:T(8,128)(2,1)S(1)} all-gather(bf16[1,256,128]{2,1,0:T(8,128)(2,1)S(1)} %get-tuple-element.14), channel_id=2, replica_groups=mesh['prow'=4,'pcol'=8] {'pcol'}, dimensions={1}, use_global_device_ids=true | all-gather | bytes 589824 | tf_op jit(solution)/shard_map/all_gather | solution.py:31
  38.0 31.6 %all-gather.2 = bf16[1,2048,128]{2,1,0:T(8,128)(2,1)S(1)} all-gather(bf16[1,256,128]{2,1,0:T(8,128)(2,1)S(1)} %get-tuple-element.15), channel_id=4, replica_groups=mesh['prow'=4,'pcol'=8] {'pcol'}, dimensions={1}, use_global_device_ids=true | all-gather | bytes 589824 | tf_op jit(solution)/shard_map/all_gather | solution.py:31
  69.6 0.8 select_bitcast_fusion.2
  70.4 0.8 select_bitcast_fusion
  71.2 31.1 %all-gather.1 = bf16[1,2048,128]{2,1,0:T(8,128)(2,1)S(1)} all-gather(bf16[1,256,128]{2,1,0:T(8,128)(2,1)S(1)} %get-tuple-element.16), channel_id=3, replica_groups=mesh['prow'=4,'pcol'=8] {'pcol'}, dimensions={1}, use_global_device_ids=true | all-gather | bytes 589824 | tf_op jit(solution)/shard_map/all_gather | solution.py:31
  102.3 0.8 select_bitcast_fusion.1
  103.0 0.0 all-reduce.7.cloned.1.call-update
  103.1 0.0 reduce-scatter.6.cloned.1.call-start
  103.1 39.1 %all-reduce.7.cloned.1.call-done = (bf16[1024,128]{1,0:T(8,128)(2,1)}, bf16[1024,128]{1,0:T(8,128)(2,1)}, bf16[1024,128]{1,0:T(8,128)(2,1)}) async-done(((bf16[1024,128]{1,0:T(8,128)(2,1)}, bf16[1024,128]{1,0:T(8,128)(2,1)}, bf16[1024,128]{1,0:T(8,128)(2,1)}), (bf16[1024,128]{1,0:T(8,128)(2,1)}, bf16[1024,128]{1,0:T(8,128)(2,1)}, bf16[1024,128]{1,0:T(8,128)(2,1)})) %all-reduce.7.cloned.1.call-update) | async-done | bytes 786448 | tf_op jit(solution)/shard_map/psum | solution.py:9
  142.2 0.0 copy-start.3
  142.2 4.8 convolution_bitcast_fusion.1
  147.0 0.0 copy-start.2
  147.0 0.0 reduce-scatter.6.cloned.1.call-update
  147.0 0.0 reduce-scatter.4.cloned.1.call-start
  147.1 0.0 copy-done.3
  147.1 4.7 convolution_bitcast_fusion.2
  151.8 0.0 copy-start
  151.8 0.0 reduce-scatter.4.cloned.1.call-update
  151.8 0.0 reduce-scatter.8.cloned.1.call-start
  151.9 0.0 copy-done.2
  151.9 0.0 copy-start.1
  151.9 4.8 convolution_bitcast_fusion
  156.7 0.0 reduce-scatter.8.cloned.1.call-update
  156.7 0.0 all-reduce.5.cloned.1.call-start
  156.7 54.9 %reduce-scatter.6.cloned.1.call-done = f32[256,128]{0,1:T(8,128)} async-done(((f32[2048,128]{0,1:T(8,128)}), f32[256,128]{0,1:T(8,128)}) %reduce-scatter.6.cloned.1.call-update) | async-done | bytes 131088 | tf_op jit(solution)/shard_map/reduce_scatter | solution.py:39
  211.7 67.1 %reduce-scatter.4.cloned.1.call-done = f32[256,128]{0,1:T(8,128)} async-done(((f32[2048,128]{0,1:T(8,128)}), f32[256,128]{0,1:T(8,128)}) %reduce-scatter.4.cloned.1.call-update) | async-done | bytes 131088 | tf_op jit(solution)/shard_map/reduce_scatter | solution.py:39
  278.8 0.0 copy-done
  278.8 1.2 fusion.2
  280.0 0.9 fusion.18
  280.9 0.8 fusion.12
  281.7 64.0 %reduce-scatter.8.cloned.1.call-done = f32[256,128]{0,1:T(8,128)} async-done(((f32[2048,128]{0,1:T(8,128)}), f32[256,128]{0,1:T(8,128)}) %reduce-scatter.8.cloned.1.call-update) | async-done | bytes 131088 | tf_op jit(solution)/shard_map/reduce_scatter | solution.py:39
  345.7 1.2 fusion.3
  346.9 0.9 fusion.14
  347.8 1.7 fusion.10
  349.5 1.8 fusion.9
  351.3 0.0 all-reduce.5.cloned.1.call-update
  351.3 0.9 fusion.11
  352.3 0.9 copy.12
  353.2 129.2 %all-reduce.5.cloned.1.call-done = (f32[128,128]{1,0:T(8,128)}, f32[128,128]{1,0:T(8,128)}, f32[128,128]{1,0:T(8,128)}, f32[128,128]{1,0:T(8,128)}, f32[128,128]{1,0:T(8,128)}) async-done(((f32[128,128]{1,0:T(8,128)}, f32[128,128]{1,0:T(8,128)}, f32[128,128]{1,0:T(8,128)}, f32[128,128]{1,0:T(8,128)}, f32[128,128]{1,0:T(8,128)}), (f32[128,128]{1,0:T(8,128)}, f32[128,128]{1,0:T(8,128)}, f32[128,128]{1,0:T(8,128)}, ...) | async-done | bytes 327696 | tf_op jit(solution)/shard_map/psum | solution.py:62
  482.4 0.0 copy-done.1
  482.4 0.8 fusion.30
  483.2 1.0 fusion.8
  484.3 1.1 fusion.7
  485.4 1.0 fusion.6
  486.4 1.1 fusion.5
  487.5 0.7 pad_maximum_fusion.2
  488.2 0.7 pad_maximum_fusion.1
  (4 shorter events, 0.1 us)
Async XLA Ops:
  7.2 135.0 %all-reduce.7.cloned.1.call-start = ((), (), s32[]{:S(2)}) async-start(), calls=%async_computation.7 | async-start | bytes 1572864 | tf_op jit(solution)/shard_map/psum | solution.py:9
  103.1 108.6 %reduce-scatter.6.cloned.1.call-start = ((), (), s32[]{:S(2)}) async-start(), calls=%async_computation.4 | async-start | bytes 1179648 | tf_op jit(solution)/shard_map/reduce_scatter | solution.py:39
  142.2 4.9 copy-start.3
  147.0 4.9 copy-start.2
  147.0 131.7 %reduce-scatter.4.cloned.1.call-start = ((), (), s32[]{:S(2)}) async-start(), calls=%async_computation.3 | async-start | bytes 1179648 | tf_op jit(solution)/shard_map/reduce_scatter | solution.py:39
  151.8 127.0 %copy-start = (bf16[2,128,128]{2,1,0:T(8,128)(2,1)S(1)}, bf16[2,128,128]{2,1,0:T(8,128)(2,1)}, u32[]{:S(2)}) copy-start(bf16[2,128,128]{2,1,0:T(8,128)(2,1)} %param.9) | copy-start | bytes 196612
  151.8 193.9 %reduce-scatter.8.cloned.1.call-start = ((), (), s32[]{:S(2)}) async-start(), calls=%async_computation.5 | async-start | bytes 1179648 | tf_op jit(solution)/shard_map/reduce_scatter | solution.py:39
  151.9 330.5 %copy-start.1 = (f32[3,128,128]{2,1,0:T(8,128)S(1)}, f32[3,128,128]{2,1,0:T(8,128)}, u32[]{:S(2)}) copy-start(f32[3,128,128]{2,1,0:T(8,128)} %param.8) | copy-start | bytes 589828
  156.7 325.7 %all-reduce.5.cloned.1.call-start = ((), (), s32[]{:S(2)}) async-start(), calls=%async_computation.6 | async-start | bytes 655360 | tf_op jit(solution)/shard_map/psum | solution.py:62
Sparse Core Ops, SparseCore 0:
  103.2 38.9 all-reduce.6
  147.2 64.4 reduce-scatter.5
  215.1 63.6 reduce-scatter.3
  282.0 63.6 reduce-scatter.7
  352.4 129.9 all-reduce.4
where the time goes:
time: 496 us; the launch traced here: 495 us
  waiting for transfers between devices  354 us (71%)
  blocking collectives  91.5 us (18%)
  matrix products  27.9 us (6%)
  between operations  13.9 us (3%)
  other arithmetic  6.52 us (1%)
    reduce_scatter x3, waiting for transfers between devices, shards(): lax.psum_scatter(single_term(jnp.int32(0), seg_rows * lax.axis_size('pcol...  186 us
    psum x1, waiting for transfers between devices, shards(): own_sum, cross_sum = lax.psum((own_term, cross_term), ('prow', 'pcol'))  129 us
    all_gather x3, blocking collectives, shards(): gathered = lax.all_gather(factor[section], 'pcol', axis=0, tiled=True)  91.5 us
    psum x1, waiting for transfers between devices, broadcast(): return lax.psum(kept, axis)  39.1 us
    dot_general x3, matrix products, single_term(): return jnp.dot(ainv, panel_cols, preferred_element_type=jnp.float32)  14.3 us
  transfers between devices with their start and end apart: 5, of which 5 were waited for; matrix products, arithmetic and copies ran while one was open for 3% of the time, Pallas kernels for 0%

commit v1 on v0

--- a/solution.py
+++ b/solution.py
@@ -28,7 +28,15 @@
     owner = column * col_span // height
     products = []
     for section in range(sections):
-        gathered = lax.all_gather(factor[section], "pcol", axis=0, tiled=True)
+        ways, here = (lax.axis_size("pcol"), lax.axis_index("pcol"))
+        grown, reach = (factor[section], 1)
+        while reach < ways:
+            theirs = lax.ppermute(grown, "pcol", [(d, d ^ reach) for d in range(ways)])
+            mine_first = jnp.concatenate([grown, theirs], axis=0)
+            theirs_first = jnp.concatenate([theirs, grown], axis=0)
+            grown = jnp.where(here & reach == 0, mine_first, theirs_first)
+            reach = 2 * reach
+        gathered = grown
         wanted = lax.dynamic_slice_in_dim(gathered, offset, col_span, 0)
         received = broadcast(wanted, "prow", owner)
 

time: 496 us -> 445 us (0.90)
  blocking collectives: 91.5 us -> 0 us
  waiting for transfers between devices: 354 us -> 377 us
  starting transfers between devices: 0.21 us -> 15.6 us
    all_gather x3 -> x0, blocking collectives: 91.5 us -> none  [shards(): gathered = lax.all_gather(factor[section], 'pcol', axis=0, tiled=True)]
    ppermute x0 -> x9, waiting for transfers between devices: none -> 24.9 us  [shards(): theirs = lax.ppermute(grown, 'pcol', [(d, d ^ reach) for d in range(ways)])]
    ppermute x0 -> x9, starting transfers between devices: none -> 15.4 us  [shards(): theirs = lax.ppermute(grown, 'pcol', [(d, d ^ reach) for d in range(ways)])]
  transfers between devices with their start and end apart: 5 -> 14, of which waited for: 5 -> 11; matrix products, arithmetic and copies ran while one was open for 3% -> 4% of each run, Pallas kernels for 0% -> 0%
where the time goes in v1:
time: 445 us
  waiting for transfers between devices  377 us (85%)
  matrix products  27.9 us (6%)
  starting transfers between devices  15.6 us (4%)
  between operations  13.9 us (3%)
  other arithmetic  9.42 us (2%)
    reduce_scatter x3, waiting for transfers between devices, shards(): lax.psum_scatter(single_term(jnp.int32(0), seg_rows * lax.axis_size('pcol...  186 us
    psum x1, waiting for transfers between devices, shards(): own_sum, cross_sum = lax.psum((own_term, cross_term), ('prow', 'pcol'))  129 us
    psum x1, waiting for transfers between devices, broadcast(): return lax.psum(kept, axis)  36.7 us
    ppermute x9, waiting for transfers between devices, shards(): theirs = lax.ppermute(grown, 'pcol', [(d, d ^ reach) for d in range(ways)])  24.9 us
    ppermute x9, starting transfers between devices, shards(): theirs = lax.ppermute(grown, 'pcol', [(d, d ^ reach) for d in range(ways)])  15.4 us
    dot_general x3, matrix products, single_term(): return jnp.dot(ainv, panel_cols, preferred_element_type=jnp.float32)  14.3 us
  transfers between devices with their start and end apart: 14, of which 11 were waited for; matrix products, arithmetic and copies ran while one was open for 4% of the time, Pallas kernels for 0%

profile of v1, /device:TPU:8, one launch (start us, length us, event | category | flops | bytes accessed | tf_op | source)
XLA Modules:
  0.0 444.7 jit_solution(8191397903630953974)
XLA Ops:
  7.2 0.0 all-reduce.7.cloned.1.call-start
  7.2 0.9 fusion.46
  8.1 1.1 broadcast_multiply_fusion
  9.3 1.6 collective-permute-start
  10.8 0.5 collective-permute-start.6
  11.4 1.5 collective-permute-start.3
  12.8 1.4 collective-permute-done
  14.3 0.1 collective-permute-start.1
  14.3 1.4 collective-permute-done.6
  15.7 0.7 collective-permute-start.7
  16.5 0.0 collective-permute-done.3
  16.5 1.4 collective-permute-start.4
  17.9 2.8 collective-permute-done.1
  20.7 0.1 maximum_select_fusion
  20.8 4.5 %collective-permute-start.2 = (bf16[1024,128]{1,0:T(8,128)(2,1)S(1)}, bf16[1024,128]{1,0:T(8,128)(2,1)S(1)}, u32[]{:S(2)}, u32[]{:S(2)}) collective-permute-start(bf16[1024,128]{1,0:T(8,128)(2,1)S(1)} %maximum_select_fusion), channel_id=1, source_target_pairs={{0,4},{1,5},{2,6},{3,7},{4,0},{5,1},{6,2},{7,3},{8,12},{9,13},{10,... | collective-permute-start | bytes 786440 | tf_op jit(solution)/shard_map/ppermute | solution.py:34
  25.3 0.0 collective-permute-done.7
  25.3 0.1 maximum_select_fusion.2
  25.4 3.7 collective-permute-start.8
  29.1 0.0 collective-permute-done.4
  29.1 0.1 maximum_select_fusion.1
  29.2 1.3 collective-permute-start.5
  30.5 15.1 %collective-permute-done.2 = bf16[1024,128]{1,0:T(8,128)(2,1)S(1)} collective-permute-done((bf16[1024,128]{1,0:T(8,128)(2,1)S(1)}, bf16[1024,128]{1,0:T(8,128)(2,1)S(1)}, u32[]{:S(2)}, u32[]{:S(2)}) %collective-permute-start.2) | collective-permute-done | bytes 262176 | tf_op jit(solution)/shard_map/ppermute | solution.py:34
  45.6 1.6 fusion.19
  47.2 3.1 collective-permute-done.8
  50.3 1.6 fusion.11
  51.9 1.2 collective-permute-done.5
  53.1 1.6 fusion.15
  54.7 0.0 all-reduce.7.cloned.1.call-update
  54.7 0.0 reduce-scatter.6.cloned.1.call-start
  54.8 36.7 %all-reduce.7.cloned.1.call-done = (bf16[1024,128]{1,0:T(8,128)(2,1)}, bf16[1024,128]{1,0:T(8,128)(2,1)}, bf16[1024,128]{1,0:T(8,128)(2,1)}) async-done(((bf16[1024,128]{1,0:T(8,128)(2,1)}, bf16[1024,128]{1,0:T(8,128)(2,1)}, bf16[1024,128]{1,0:T(8,128)(2,1)}), (bf16[1024,128]{1,0:T(8,128)(2,1)}, bf16[1024,128]{1,0:T(8,128)(2,1)}, bf16[1024,128]{1,0:T(8,128)(2,1)})) %all-reduce.7.cloned.1.call-update) | async-done | bytes 786448 | tf_op jit(solution)/shard_map/psum | solution.py:9
  91.5 4.8 %convolution_bitcast_fusion.1 = f32[2048,128]{0,1:T(8,128)} fusion(bf16[1024,128]{1,0:T(8,128)(2,1)} %get-tuple-element.12, bf16[2048,1024]{1,0:T(8,128)(2,1)} %param.5), kind=kOutput, calls=%fused_computation.1 | convolution fusion | flops 536870912 | bytes 5505024 | tf_op jit(solution)/shard_map/dot_general | solution.py:44
  96.3 0.0 reduce-scatter.6.cloned.1.call-update
  96.3 0.0 reduce-scatter.4.cloned.1.call-start
  96.4 0.0 copy-done.3
  96.4 4.7 %convolution_bitcast_fusion.2 = f32[2048,128]{0,1:T(8,128)} fusion(bf16[1024,128]{1,0:T(8,128)(2,1)S(1)} %copy-done.3, bf16[2048,1024]{1,0:T(8,128)(2,1)} %param.5), kind=kOutput, calls=%fused_computation.2 | convolution fusion | flops 536870912 | bytes 5505024 | tf_op jit(solution)/shard_map/dot_general | solution.py:44
  101.1 0.0 reduce-scatter.4.cloned.1.call-update
  101.1 0.0 reduce-scatter.8.cloned.1.call-start
  101.1 0.0 copy-done.2
  101.2 0.0 copy-start.1
  101.2 4.7 %convolution_bitcast_fusion = f32[2048,128]{0,1:T(8,128)} fusion(bf16[1024,128]{1,0:T(8,128)(2,1)S(1)} %copy-done.2, bf16[2048,1024]{1,0:T(8,128)(2,1)} %param.5), kind=kOutput, calls=%fused_computation | convolution fusion | flops 536870912 | bytes 5505024 | tf_op jit(solution)/shard_map/dot_general | solution.py:44
  105.9 0.0 reduce-scatter.8.cloned.1.call-update
  105.9 0.0 all-reduce.5.cloned.1.call-start
  106.0 55.0 %reduce-scatter.6.cloned.1.call-done = f32[256,128]{0,1:T(8,128)} async-done(((f32[2048,128]{0,1:T(8,128)}), f32[256,128]{0,1:T(8,128)}) %reduce-scatter.6.cloned.1.call-update) | async-done | bytes 131088 | tf_op jit(solution)/shard_map/reduce_scatter | solution.py:47
  160.9 67.2 %reduce-scatter.4.cloned.1.call-done = f32[256,128]{0,1:T(8,128)} async-done(((f32[2048,128]{0,1:T(8,128)}), f32[256,128]{0,1:T(8,128)}) %reduce-scatter.4.cloned.1.call-update) | async-done | bytes 131088 | tf_op jit(solution)/shard_map/reduce_scatter | solution.py:47
  228.1 0.0 copy-done
  228.1 1.2 fusion.2
  229.4 0.9 fusion.42
  230.2 0.8 fusion.43
  231.1 64.0 %reduce-scatter.8.cloned.1.call-done = f32[256,128]{0,1:T(8,128)} async-done(((f32[2048,128]{0,1:T(8,128)}), f32[256,128]{0,1:T(8,128)}) %reduce-scatter.8.cloned.1.call-update) | async-done | bytes 131088 | tf_op jit(solution)/shard_map/reduce_scatter | solution.py:47
  295.1 1.2 fusion.3
  296.2 0.9 fusion.44
  297.1 1.7 fusion.22
  298.9 1.8 fusion.21
  300.6 0.0 all-reduce.5.cloned.1.call-update
  300.7 0.9 fusion.23
  301.6 0.9 copy.12
  302.5 129.2 %all-reduce.5.cloned.1.call-done = (f32[128,128]{1,0:T(8,128)}, f32[128,128]{1,0:T(8,128)}, f32[128,128]{1,0:T(8,128)}, f32[128,128]{1,0:T(8,128)}, f32[128,128]{1,0:T(8,128)}) async-done(((f32[128,128]{1,0:T(8,128)}, f32[128,128]{1,0:T(8,128)}, f32[128,128]{1,0:T(8,128)}, f32[128,128]{1,0:T(8,128)}, f32[128,128]{1,0:T(8,128)}), (f32[128,128]{1,0:T(8,128)}, f32[128,128]{1,0:T(8,128)}, f32[128,128]{1,0:T(8,128)}, ...) | async-done | bytes 327696 | tf_op jit(solution)/shard_map/psum | solution.py:70
  431.7 0.8 fusion.34
  432.6 1.0 fusion.8
  433.6 1.1 fusion.7
  434.7 1.0 fusion.6
  435.7 1.1 fusion.5
  436.8 0.7 pad_maximum_fusion.2
  437.5 0.7 pad_maximum_fusion.1
  (11 shorter events, 0.2 us)
Async XLA Ops:
  7.2 84.3 %all-reduce.7.cloned.1.call-start = ((), (), s32[]{:S(2)}) async-start(), calls=%async_computation.7 | async-start | bytes 1572864 | tf_op jit(solution)/shard_map/psum | solution.py:9
  9.3 5.0 %collective-permute-start = (bf16[256,128]{1,0:T(8,128)(2,1)S(1)}, bf16[256,128]{1,0:T(8,128)(2,1)S(1)}, u32[]{:S(2)}, u32[]{:S(2)}) collective-permute-start(bf16[256,128]{1,0:T(8,128)(2,1)S(1)} %get-tuple-element.14), channel_id=1, source_target_pairs={{0,1},{1,0},{2,3},{3,2},{4,5},{5,4},{6,7},{7,6},{8,9},{9,8},{10,11... | collective-permute-start | bytes 196616 | tf_op jit(solution)/shard_map/ppermute | solution.py:34
  10.8 4.9 %collective-permute-start.6 = (bf16[256,128]{1,0:T(8,128)(2,1)S(1)}, bf16[256,128]{1,0:T(8,128)(2,1)S(1)}, u32[]{:S(2)}, u32[]{:S(2)}) collective-permute-start(bf16[256,128]{1,0:T(8,128)(2,1)S(1)} %get-tuple-element.15), channel_id=1, source_target_pairs={{0,1},{1,0},{2,3},{3,2},{4,5},{5,4},{6,7},{7,6},{8,9},{9,8},{10,11... | collective-permute-start | bytes 196616 | tf_op jit(solution)/shard_map/ppermute | solution.py:34
  11.4 5.1 %collective-permute-start.3 = (bf16[256,128]{1,0:T(8,128)(2,1)S(1)}, bf16[256,128]{1,0:T(8,128)(2,1)S(1)}, u32[]{:S(2)}, u32[]{:S(2)}) collective-permute-start(bf16[256,128]{1,0:T(8,128)(2,1)S(1)} %get-tuple-element.16), channel_id=1, source_target_pairs={{0,1},{1,0},{2,3},{3,2},{4,5},{5,4},{6,7},{7,6},{8,9},{9,8},{10,11... | collective-permute-start | bytes 196616 | tf_op jit(solution)/shard_map/ppermute | solution.py:34
  14.3 6.4 %collective-permute-start.1 = (bf16[512,128]{1,0:T(8,128)(2,1)S(1)}, bf16[512,128]{1,0:T(8,128)(2,1)S(1)}, u32[]{:S(2)}, u32[]{:S(2)}) collective-permute-start(bf16[512,128]{1,0:T(8,128)(2,1)S(1)} %maximum_select_fusion.3), channel_id=1, source_target_pairs={{0,2},{1,3},{2,0},{3,1},{4,6},{5,7},{6,4},{7,5},{8,10},{9,11},{10,... | collective-permute-start | bytes 393224 | tf_op jit(solution)/shard_map/ppermute | solution.py:34
  15.7 9.6 %collective-permute-start.7 = (bf16[512,128]{1,0:T(8,128)(2,1)S(1)}, bf16[512,128]{1,0:T(8,128)(2,1)S(1)}, u32[]{:S(2)}, u32[]{:S(2)}) collective-permute-start(bf16[512,128]{1,0:T(8,128)(2,1)S(1)} %maximum_select_fusion.5), channel_id=1, source_target_pairs={{0,2},{1,3},{2,0},{3,1},{4,6},{5,7},{6,4},{7,5},{8,10},{9,11},{10,... | collective-permute-start | bytes 393224 | tf_op jit(solution)/shard_map/ppermute | solution.py:34
  16.5 12.6 %collective-permute-start.4 = (bf16[512,128]{1,0:T(8,128)(2,1)S(1)}, bf16[512,128]{1,0:T(8,128)(2,1)S(1)}, u32[]{:S(2)}, u32[]{:S(2)}) collective-permute-start(bf16[512,128]{1,0:T(8,128)(2,1)S(1)} %maximum_select_fusion.4), channel_id=1, source_target_pairs={{0,2},{1,3},{2,0},{3,1},{4,6},{5,7},{6,4},{7,5},{8,10},{9,11},{10,... | collective-permute-start | bytes 393224 | tf_op jit(solution)/shard_map/ppermute | solution.py:34
  20.8 24.8 %collective-permute-start.2 = (bf16[1024,128]{1,0:T(8,128)(2,1)S(1)}, bf16[1024,128]{1,0:T(8,128)(2,1)S(1)}, u32[]{:S(2)}, u32[]{:S(2)}) collective-permute-start(bf16[1024,128]{1,0:T(8,128)(2,1)S(1)} %maximum_select_fusion), channel_id=1, source_target_pairs={{0,4},{1,5},{2,6},{3,7},{4,0},{5,1},{6,2},{7,3},{8,12},{9,13},{10,... | collective-permute-start | bytes 786440 | tf_op jit(solution)/shard_map/ppermute | solution.py:34
  25.4 24.9 %collective-permute-start.8 = (bf16[1024,128]{1,0:T(8,128)(2,1)S(1)}, bf16[1024,128]{1,0:T(8,128)(2,1)S(1)}, u32[]{:S(2)}, u32[]{:S(2)}) collective-permute-start(bf16[1024,128]{1,0:T(8,128)(2,1)S(1)} %maximum_select_fusion.2), channel_id=1, source_target_pairs={{0,4},{1,5},{2,6},{3,7},{4,0},{5,1},{6,2},{7,3},{8,12},{9,13},{10,... | collective-permute-start | bytes 786440 | tf_op jit(solution)/shard_map/ppermute | solution.py:34
  29.2 23.9 %collective-permute-start.5 = (bf16[1024,128]{1,0:T(8,128)(2,1)S(1)}, bf16[1024,128]{1,0:T(8,128)(2,1)S(1)}, u32[]{:S(2)}, u32[]{:S(2)}) collective-permute-start(bf16[1024,128]{1,0:T(8,128)(2,1)S(1)} %maximum_select_fusion.1), channel_id=1, source_target_pairs={{0,4},{1,5},{2,6},{3,7},{4,0},{5,1},{6,2},{7,3},{8,12},{9,13},{10,... | collective-permute-start | bytes 786440 | tf_op jit(solution)/shard_map/ppermute | solution.py:34
  54.7 106.2 %reduce-scatter.6.cloned.1.call-start = ((), (), s32[]{:S(2)}) async-start(), calls=%async_computation.4 | async-start | bytes 1179648 | tf_op jit(solution)/shard_map/reduce_scatter | solution.py:47
  91.5 4.9 %copy-start.3 = (bf16[1024,128]{1,0:T(8,128)(2,1)S(1)}, bf16[1024,128]{1,0:T(8,128)(2,1)}, u32[]{:S(2)}) copy-start(bf16[1024,128]{1,0:T(8,128)(2,1)} %get-tuple-element.13) | copy-start | bytes 786436
  96.3 4.9 %copy-start.2 = (bf16[1024,128]{1,0:T(8,128)(2,1)S(1)}, bf16[1024,128]{1,0:T(8,128)(2,1)}, u32[]{:S(2)}) copy-start(bf16[1024,128]{1,0:T(8,128)(2,1)} %get-tuple-element.11) | copy-start | bytes 786436
  96.3 131.8 %reduce-scatter.4.cloned.1.call-start = ((), (), s32[]{:S(2)}) async-start(), calls=%async_computation.3 | async-start | bytes 1179648 | tf_op jit(solution)/shard_map/reduce_scatter | solution.py:47
  101.1 127.1 %copy-start = (bf16[2,128,128]{2,1,0:T(8,128)(2,1)S(1)}, bf16[2,128,128]{2,1,0:T(8,128)(2,1)}, u32[]{:S(2)}) copy-start(bf16[2,128,128]{2,1,0:T(8,128)(2,1)} %param.9) | copy-start | bytes 196612
  101.1 194.0 %reduce-scatter.8.cloned.1.call-start = ((), (), s32[]{:S(2)}) async-start(), calls=%async_computation.5 | async-start | bytes 1179648 | tf_op jit(solution)/shard_map/reduce_scatter | solution.py:47
  101.2 330.6 %copy-start.1 = (f32[3,128,128]{2,1,0:T(8,128)S(1)}, f32[3,128,128]{2,1,0:T(8,128)}, u32[]{:S(2)}) copy-start(f32[3,128,128]{2,1,0:T(8,128)} %param.8) | copy-start | bytes 589828
  105.9 325.8 %all-reduce.5.cloned.1.call-start = ((), (), s32[]{:S(2)}) async-start(), calls=%async_computation.6 | async-start | bytes 655360 | tf_op jit(solution)/shard_map/psum | solution.py:70
Sparse Core Ops, SparseCore 0:
  54.9 36.5 all-reduce.6
  96.4 64.4 reduce-scatter.5
  164.4 63.7 reduce-scatter.3
  231.4 63.6 reduce-scatter.7
  301.7 129.9 all-reduce.4
